TPU v7x, 256 devices: a whole 4x4x8 slice. The times are simulated.
256 devices in a mesh: grp: 8 (over x, core), dev: 32 (over y, z).
Axes of the slice: x: 4, y: 4, z: 8, core: 2. Of those that a mesh axis runs over, the one named last changes fastest.
Arguments:
- residual: bfloat16 [256, 524288], P('dev', 'grp'), may hold values from -6 to 6
- coefficients: bfloat16 [256, 128], replicated, may hold values from -0.375 to 0.375
- slot_ray: int32 [8, 32, 8, 16], P('grp', 'dev'), may hold values from 0 to 15
- slot_vox: int32 [8, 32, 8, 16], P('grp', 'dev'), may hold values from 0 to 511, as said below
- slot_count: int32 [8, 32, 8], P('grp', 'dev'), may hold values from 8 to 16, as said below
- footprint: bfloat16 [8, 32, 8, 16, 128, 128], P('grp', 'dev'), may hold values from -0.5 to 0.5
Outputs:
- basis_grad: float32 [524288, 128], P(('grp', 'dev'))
Inputs may be any that keep to these rules, and one draw needn't show every extreme that they name: For each dev index d and destination group h, the 128 slots slot_vox[:, d, h, :] (used or not) name blocks of any one device of group h (blocks j * 16 to j * 16 + 15) at most 4 times. `slot_count`: every device has a list to some group with all 16 slots used.
All inputs are finite; a program needn't handle non-finite values.
Results may differ from a plain program's by a relative error of at most 0.0041.
Values may be sent and summed in bfloat16 or wider, within the bound.
No kernel may reach another device: no remote copies, remote signals or barrier semaphores. Data moves between devices by JAX's collectives and lax.ppermute only.
A program may use at most 128 MiB of HBM per device.

v0:
```python
import functools

import jax
import jax.numpy as jnp
from jax import lax
from jax.experimental import pallas as pl
from jax.experimental.pallas import tpu as pltpu
from jax.sharding import PartitionSpec as P


BLK = 128
CAP = 16
CORES = 2
NX = 4
NY = 4
NZ = 8
VB = 16
PART = CORES * CAP
CHUNKS = (32, 48, 48)
HOPS = NZ // 2
VMEM_LIMIT = 10 << 20
RINGS = ((0, 1), (2,))


VMEM = pl.BlockSpec(memory_space=pltpu.VMEM)
SMEM = pl.BlockSpec(memory_space=pltpu.SMEM)


def call(kernel, out_shape, ins, smems, flops=0, scratch=()):
    specs = [SMEM] * smems + [VMEM] * (len(ins) - smems)
    many = isinstance(out_shape, list)
    return pl.pallas_call(
        kernel,
        out_shape=out_shape,
        in_specs=specs,
        out_specs=[VMEM] * len(out_shape) if many else VMEM,
        scratch_shapes=list(scratch),
        compiler_params=pltpu.CompilerParams(vmem_limit_bytes=VMEM_LIMIT),
        cost_estimate=pl.CostEstimate(flops=flops, bytes_accessed=4 << 20, transcendentals=0),
    )(*ins)


def adjoint_kernel(rows, rays_ref, place_ref, own_ref, par_ref, fpo_ref, fpr_ref, *outs):
    low, high = rows[0][0], rows[-1][1]
    size = high - low
    blank = jnp.zeros((size, BLK), jnp.bfloat16)
    for k in range(NX):
        to = lax.rem(place_ref[0] + k, NX)
        for side, (proj, tiles) in enumerate(((own_ref, fpo_ref), (par_ref, fpr_ref))):

            for quad in range(CAP // 4):
                first = (k * CORES + side) * CAP + quad * 4
                stack = []
                for v in range(4):
                    ray = rays_ref[first + v]
                    rank = proj[low:high, pl.ds(pl.multiple_of(jnp.maximum(ray, 0) * BLK, BLK), BLK)]
                    rank = jnp.where(ray >= 0, rank, blank)
                    stack.append(jnp.concatenate([blank, rank] if v % 2 else [rank, blank], axis=1))
                made = jnp.dot(
                    jnp.concatenate(stack, axis=0),
                    jnp.concatenate([tiles[to, quad * 2], tiles[to, quad * 2 + 1]], axis=1),
                    preferred_element_type=jnp.float32,
                )
                for v in range(4):
                    block = made[v * size : (v + 1) * size, (v // 2) * BLK : (v // 2 + 1) * BLK].astype(jnp.bfloat16)
                    for j, (lo, hi) in enumerate(rows):
                        outs[j * NX + k][side * CAP + quad * 4 + v] = block[lo - low : hi - low]


def pack_kernel(src_ref, *refs):
    ins, outs, buf = refs[:NX], refs[NX : NX + NY], refs[NX + NY]
    for k in range(NX):
        buf[k * PART : (k + 1) * PART] = ins[k][...]
    for k in range(NY):

        def move(i, carry, k=k):
            for u in range(8):
                p = i * 8 + u
                outs[k][p] = buf[src_ref[k * PART + p]]
            return carry

        lax.fori_loop(0, PART // 8, move, 0)


def gather_kernel(up_far, earlier, at_ref, *refs):
    ins, before, dense = refs[:NY], refs[NY : NY + earlier], refs[NY + earlier]
    sends = refs[NY + earlier + 1 :]
    dense[...] = jnp.zeros_like(dense)
    for k in range(NY):

        def add(i, carry, k=k):
            for u in range(4):
                p = i * 4 + u
                at = at_ref[k * PART + p]
                dense[at] = dense[at] + ins[k][p].astype(jnp.float32)
            return carry

        lax.fori_loop(0, PART // 4, add, 0)
    for send, far in zip(sends, (up_far, up_far + 1)):
        low = 0
        for part in tuple(before) + (dense,):
            high = low + part.shape[1]
            send[:, low:high, :] = part[far * VB : (far + 1) * VB].astype(jnp.bfloat16)
            low = high


def hop_kernel(places, count, *refs):
    dense, refs = refs[:count], refs[count:]
    n = len(places)
    for came, goes, at in zip(refs[:n], refs[n:], places):
        low = 0
        for part in dense:
            high = low + part.shape[1]
            mine = part[at * VB : (at + 1) * VB]
            goes[:, low:high, :] = (came[:, low:high, :].astype(jnp.float32) + mine).astype(jnp.bfloat16)
            low = high


def finish_kernel(groups, *refs):
    parts, out = refs[:-1], refs[-1]
    for b in range(VB):
        rows, at = [], 0
        for group in groups:
            up, down = parts[at + len(group)], parts[at + len(group) + 1]
            low = 0
            for part in parts[at : at + len(group)]:
                high = low + part.shape[1]
                rows.append(
                    part[b] + up[b, low:high, :].astype(jnp.float32) + down[b, low:high, :].astype(jnp.float32)
                )
                low = high
            at += len(group) + 2
        out[b * BLK : (b + 1) * BLK, :] = jnp.concatenate(rows, axis=0).T


def x_shift(k):
    return [(x * CORES + c, (x + k) % NX * CORES + c) for x in range(NX) for c in range(CORES)]


def core_swap():
    return [(g, g ^ 1) for g in range(NX * CORES)]


def y_shift(k):
    return [(y * NZ + z, (y + k) % NY * NZ + z) for y in range(NY) for z in range(NZ)]


def z_shift(k):
    return [(y * NZ + z, y * NZ + (z + k) % NZ) for y in range(NY) for z in range(NZ)]


def exchange(parts, axis, shift):
    moved = [parts[0]]
    for k in range(1, len(parts)):
        moved.append(lax.ppermute(parts[k], axis, shift(k)))
    return moved


def spread(known, axis, near):
    for pairs in near:
        known = jnp.concatenate([known, lax.ppermute(known, axis, pairs)], axis=0)
    return known


def flip(size, unit, bit):
    return [(i, i ^ (bit * unit)) for i in range(size)]


def routes(slot_ray, slot_vox, slot_count, x, c, y, z):
    used = jnp.arange(CAP, dtype=jnp.int32)[None, :] < slot_count[:, None]
    lists = jnp.concatenate([jnp.where(used, slot_ray, -1), slot_vox], axis=1)
    size = NX * CORES
    near = [flip(size, 1, 1), flip(size, CORES, 1), flip(size, CORES, 2)]
    table = spread(lists[None], "grp", near)
    table = table.reshape(NX, CORES, NX, CORES, 2 * CAP)
    mine = lax.dynamic_index_in_dim(table, c, 3, keepdims=False)
    rays = lax.dynamic_slice_in_dim(jnp.concatenate([mine[0]] * 2, axis=1), x, NX, 1)
    rays = jnp.transpose(rays, (1, 0, 2))[:, :, :CAP].reshape(NX * PART)
    vox = lax.dynamic_index_in_dim(mine, x, 2, keepdims=False)[:, :, CAP:].reshape(NX, PART)
    entry = jnp.bitwise_xor(x, lax.rem(x - jnp.arange(NX, dtype=jnp.int32) + NX, NX))
    pick = (entry[:, None] == jnp.arange(NX, dtype=jnp.int32)[None, :]).astype(jnp.int32)
    vox = jnp.sum(pick[:, :, None] * vox[None], axis=1).reshape(1, NX * PART)
    near = [flip(NY * NZ, NZ, 1), flip(NY * NZ, NZ, 2)]
    vox = spread(vox, "dev", near)
    key = lax.rem(vox // (NZ * VB), NY)
    there = jnp.bitwise_xor(y, jnp.arange(NY, dtype=jnp.int32))
    turn = lax.rem(key - there[:, None] + NY, NY)
    slots = jnp.arange(NX * PART, dtype=jnp.int32)
    same = (turn[:, :, None] == turn[:, None, :]) & (slots[None, None, :] < slots[None, :, None])
    target = turn * PART + jnp.sum(same.astype(jnp.int32), axis=2)
    hit = (target[:, None, :] == slots[None, :, None]).astype(jnp.int32)
    src = jnp.sum(hit[0] * slots[None, :], axis=1)
    place = lax.rem(lax.rem(vox // VB, NZ) - z + NZ, NZ) * VB + lax.rem(vox, VB)
    at = jnp.sum(hit * place[:, None, :], axis=2).reshape(NY, NY, PART)
    entry = jnp.bitwise_xor(y, lax.rem(y - jnp.arange(NY, dtype=jnp.int32) + NY, NY))
    pick = (entry[:, None] == jnp.arange(NY, dtype=jnp.int32)[None, :]).astype(jnp.int32)
    at = jnp.sum(pick[:, :, None] * jnp.transpose(at, (1, 0, 2)), axis=1).reshape(NY * PART)
    return rays, src, at


def turns(r):
    up_far = HOPS - r % 2
    return list(range(up_far, 0, -1)), list(range(up_far + 1, NZ))


def ring(r, dense, up, down):
    ups, downs = turns(r)
    for hop in range(HOPS):
        sent = []
        for part, far, step in ((up, ups, 1), (down, downs, NZ - 1)):
            if hop < len(far):
                part = lax.ppermute(part, "dev", z_shift(step))
            sent.append(part)
        up, down = sent
        places = [far[hop + 1] for far in (ups, downs) if hop + 1 < len(far)]
        if places:
            going = [part for part, far in ((up, ups), (down, downs)) if hop + 1 < len(far)]
            going = call(
                functools.partial(hop_kernel, places, len(dense)),
                [pltpu.VMEM(part.shape, part.dtype) for part in going],
                dense + going,
                0,
            )
            up = going[0] if hop + 1 < len(ups) else up
            down = going[-1] if hop + 1 < len(downs) else down
    return dense + [up, down]


def body(residual, coefficients, slot_ray, slot_vox, slot_count, footprint):
    g, d = lax.axis_index("grp"), lax.axis_index("dev")
    x, c, y, z = g // CORES, g % CORES, d // NZ, d % NZ
    panel = lax.all_to_all(residual, "dev", split_axis=1, concat_axis=0, tiled=True)
    tables = routes(slot_ray[0, 0], slot_vox[0, 0], slot_count[0, 0], x, c, y, z)
    place = jnp.stack([x, c]).astype(jnp.int32)
    tiles = footprint.reshape(NX, CORES, CAP // 2, 2 * BLK, BLK)
    fpo = lax.dynamic_index_in_dim(tiles, c, 1, keepdims=False)
    fpr = lax.dynamic_index_in_dim(tiles, 1 - c, 1, keepdims=False)
    fpr = lax.ppermute(fpr, "grp", core_swap())
    panel, (rays, src, at), place, fpo, fpr = lax.optimization_barrier((panel, tables, place, fpo, fpr))
    own = lax.dot_general(
        coefficients, panel, (((0,), (0,)), ((), ())), preferred_element_type=jnp.float32
    ).astype(jnp.bfloat16)
    par = lax.ppermute(own, "grp", core_swap())
    rows = [(sum(CHUNKS[:i]), sum(CHUNKS[: i + 1])) for i in range(len(CHUNKS))]
    made = []
    for some in (rows[:1], rows[1:]):
        made += call(
            functools.partial(adjoint_kernel, some),
            [pltpu.VMEM((PART, hi - lo, BLK), jnp.bfloat16) for lo, hi in some for _ in range(NX)],
            [rays, place, own, par, fpo, fpr],
            2,
        )
    ends = []
    for r, group in enumerate(RINGS):
        dense = []
        for i in group:
            size = CHUNKS[i]
            block = pltpu.VMEM((PART, size, BLK), jnp.bfloat16)
            parts = exchange(made[i * NX : (i + 1) * NX], "grp", x_shift)
            parts = call(
                pack_kernel, [block] * NY, [src] + parts, 1, scratch=[pltpu.VMEM((NX * PART, size, BLK), jnp.bfloat16)]
            )
            parts = exchange(parts, "dev", y_shift)
            sends = []
            if i == group[-1]:
                sends = [pltpu.VMEM((VB, sum(CHUNKS[j] for j in group), BLK), jnp.bfloat16)] * 2
            before = dense if sends else []
            came = call(
                functools.partial(gather_kernel, turns(r)[0][0], len(before)),
                [pltpu.VMEM((NZ * VB, size, BLK), jnp.float32)] + sends,
                [at] + parts + before,
                1,
            )
            dense = dense + [came[0]]
        ends += ring(r, dense, came[1], came[2])
    return call(functools.partial(finish_kernel, RINGS), jax.ShapeDtypeStruct((VB * BLK, BLK), jnp.float32), ends, 0)


def solution(mesh):
    placed = (
        P("dev", "grp"),
        P(),
        P("grp", "dev", None, None),
        P("grp", "dev", None, None),
        P("grp", "dev", None),
        P("grp", "dev", None, None, None, None),
    )

    return jax.shard_map(body, mesh=mesh, in_specs=placed, out_specs=P(("grp", "dev"), None), check_vma=False)
```

profile of v0, /device:TPU:10, one launch (start us, length us, event | category | flops | bytes accessed | tf_op | source)
XLA Modules:
  0.0 177.3 jit_solution(8396427962083938933)
XLA Ops:
  0.0 11.8 %all-to-all-start = ((bf16[8,32,2048]{2,0,1:T(8,128)(2,1)}), bf16[8,32,2048]{2,0,1:T(8,128)(2,1)S(1)}, u32[]{:S(2)}, u32[]{:S(2)}) async-start(bf16[8,32,2048]{2,0,1:T(8,128)(2,1)} %bitcast.43), calls=%async_computation | async-start | bytes 2097152 | tf_op jit(solution)/shard_map/all_to_all | solution.py:232
  12.1 4.0 %dynamic-slice_bitcast_fusion = (bf16[4,8,256,128]{3,2,1,0:T(8,128)(2,1)}, bf16[4,8,256,128]{3,2,1,0:T(8,128)(2,1)S(1)}) fusion(bf16[4,2,8,256,128]{4,3,2,1,0:T(8,128)(2,1)} %bitcast.41, s32[]{:T(128)S(6)} %select_n.77, s32[]{:T(128)S(6)} %select_n.67), kind=kLoop, calls=%fused_computation.2 | loop fusion | bytes 8388616 | tf_op jit(solution)/shard_map/jit(dynamic_index_in_dim)/squeeze | solution.py:237
  17.3 3.1 %collective-permute-done.1 = s32[2,8,32]{2,1,0:T(8,128)S(1)} collective-permute-done((s32[2,8,32]{2,1,0:T(8,128)S(1)}, s32[2,8,32]{2,1,0:T(8,128)S(1)}, u32[]{:S(2)}, u32[]{:S(2)}) %collective-permute-start.1) | collective-permute-done | bytes 2080 | tf_op jit(solution)/shard_map/ppermute | solution.py:161
  22.6 3.0 %collective-permute-done.2 = s32[4,8,32]{2,1,0:T(8,128)S(1)} collective-permute-done((s32[4,8,32]{2,1,0:T(8,128)S(1)}, s32[4,8,32]{2,1,0:T(8,128)S(1)}, u32[]{:S(2)}, u32[]{:S(2)}) %collective-permute-start.2) | collective-permute-done | bytes 4128 | tf_op jit(solution)/shard_map/ppermute | solution.py:161
  26.3 3.3 %collective-permute-done.3 = s32[1,128]{1,0:T(1,128)S(1)} collective-permute-done((s32[1,128]{1,0:T(1,128)S(1)}, s32[1,128]{1,0:T(1,128)S(1)}, u32[]{:S(2)}, u32[]{:S(2)}) %collective-permute-start.3) | collective-permute-done | bytes 544 | tf_op jit(solution)/shard_map/ppermute | solution.py:161
  31.8 2.9 %collective-permute-done.4 = s32[2,128]{1,0:T(2,128)S(1)} collective-permute-done((s32[2,128]{1,0:T(2,128)S(1)}, s32[2,128]{1,0:T(2,128)S(1)}, u32[]{:S(2)}, u32[]{:S(2)}) %collective-permute-start.4) | collective-permute-done | bytes 1056 | tf_op jit(solution)/shard_map/ppermute | solution.py:161
  40.3 3.4 %shard_map.67 = (bf16[32,48,128]{2,1,0:T(8,128)(2,1)S(1)}, bf16[32,48,128]{2,1,0:T(8,128)(2,1)S(1)}, bf16[32,48,128]{2,1,0:T(8,128)(2,1)S(1)}, bf16[32,48,128]{2...) custom-call(s32[128]{0:T(128)S(1)} %reshape.475.rays_ref, ...), custom_call_target="tpu_custom_call" | custom-call | bytes 4194304 | tf_op jit(solution)/shard_map/pallas_call | solution.py:32
  51.1 3.5 %collective-permute-start.8 = (bf16[32,32,128]{2,1,0:T(8,128)(2,1)S(1)}, bf16[32,32,128]{2,1,0:T(8,128)(2,1)S(1)}, u32[]{:S(2)}, u32[]{:S(2)}) collective-permute-start(bf16[32,32,128]{2,1,0:T(8,128)(2,1)S(1)} %get-tuple-element.59), channel_id=1, source_target_pairs={{0,128},{32,160},{64,192},{96,224},{128,0},{160,32},{192,64},{224,... | collective-permute-start | bytes 786440 | tf_op jit(solution)/shard_map/ppermute | solution.py:155
  54.6 8.1 %collective-permute-done.13.refs_1_ = bf16[32,48,128]{2,1,0:T(8,128)(2,1)S(1)} collective-permute-done((bf16[32,48,128]{2,1,0:T(8,128)(2,1)S(1)}, bf16[32,48,128]{2,1,0:T(8,128)(2,1)S(1)}, u32[]{:S(2)}, u32[]{:S(2)}) %collective-permute-start.13) | collective-permute-done | bytes 393248 | tf_op jit(solution)/shard_map/ppermute | solution.py:155
  62.8 4.6 %collective-permute-done.15.refs_3_ = bf16[32,48,128]{2,1,0:T(8,128)(2,1)S(1)} collective-permute-done((bf16[32,48,128]{2,1,0:T(8,128)(2,1)S(1)}, bf16[32,48,128]{2,1,0:T(8,128)(2,1)S(1)}, u32[]{:S(2)}, u32[]{:S(2)}) %collective-permute-start.15) | collective-permute-done | bytes 393248 | tf_op jit(solution)/shard_map/ppermute | solution.py:155
  69.9 3.0 %collective-permute-done.8.refs_2_ = bf16[32,32,128]{2,1,0:T(8,128)(2,1)S(1)} collective-permute-done((bf16[32,32,128]{2,1,0:T(8,128)(2,1)S(1)}, bf16[32,32,128]{2,1,0:T(8,128)(2,1)S(1)}, u32[]{:S(2)}, u32[]{:S(2)}) %collective-permute-start.8) | collective-permute-done | bytes 262176 | tf_op jit(solution)/shard_map/ppermute | solution.py:155
  72.9 3.8 %collective-permute-done.9.refs_3_ = bf16[32,32,128]{2,1,0:T(8,128)(2,1)S(1)} collective-permute-done((bf16[32,32,128]{2,1,0:T(8,128)(2,1)S(1)}, bf16[32,32,128]{2,1,0:T(8,128)(2,1)S(1)}, u32[]{:S(2)}, u32[]{:S(2)}) %collective-permute-start.9) | collective-permute-done | bytes 262176 | tf_op jit(solution)/shard_map/ppermute | solution.py:155
  79.1 3.3 %collective-permute-start.11 = (bf16[32,32,128]{2,1,0:T(8,128)(2,1)S(1)}, bf16[32,32,128]{2,1,0:T(8,128)(2,1)S(1)}, u32[]{:S(2)}, u32[]{:S(2)}) collective-permute-start(bf16[32,32,128]{2,1,0:T(8,128)(2,1)S(1)} %get-tuple-element.63), channel_id=1, source_target_pairs={{0,16},{1,17},{2,18},{3,19},{4,20},{5,21},{6,22},{7,23},{8,24},{9,... | collective-permute-start | bytes 786440 | tf_op jit(solution)/shard_map/ppermute | solution.py:155
  83.4 4.1 %collective-permute-done.10.refs_1_ = bf16[32,32,128]{2,1,0:T(8,128)(2,1)S(1)} collective-permute-done((bf16[32,32,128]{2,1,0:T(8,128)(2,1)S(1)}, bf16[32,32,128]{2,1,0:T(8,128)(2,1)S(1)}, u32[]{:S(2)}, u32[]{:S(2)}) %collective-permute-start.10) | collective-permute-done | bytes 262176 | tf_op jit(solution)/shard_map/ppermute | solution.py:155
  87.5 15.6 %collective-permute-start.18 = (bf16[32,48,128]{2,1,0:T(8,128)(2,1)S(1)}, bf16[32,48,128]{2,1,0:T(8,128)(2,1)S(1)}, u32[]{:S(2)}, u32[]{:S(2)}) collective-permute-start(bf16[32,48,128]{2,1,0:T(8,128)(2,1)S(1)} %get-tuple-element.72), channel_id=1, source_target_pairs={{0,24},{1,25},{2,26},{3,27},{4,28},{5,29},{6,30},{7,31},{8,0},{9,1... | collective-permute-start | bytes 1179656 | tf_op jit(solution)/shard_map/ppermute | solution.py:155
  115.2 2.5 %collective-permute-done.28.refs_3_ = bf16[32,48,128]{2,1,0:T(8,128)(2,1)S(1)} collective-permute-done((bf16[32,48,128]{2,1,0:T(8,128)(2,1)S(1)}, bf16[32,48,128]{2,1,0:T(8,128)(2,1)S(1)}, u32[]{:S(2)}, u32[]{:S(2)}) %collective-permute-start.28) | collective-permute-done | bytes 393248 | tf_op jit(solution)/shard_map/ppermute | solution.py:155
  127.1 3.5 %collective-permute-done.29.refs_1_ = bf16[32,48,128]{2,1,0:T(8,128)(2,1)S(1)} collective-permute-done((bf16[32,48,128]{2,1,0:T(8,128)(2,1)S(1)}, bf16[32,48,128]{2,1,0:T(8,128)(2,1)S(1)}, u32[]{:S(2)}, u32[]{:S(2)}) %collective-permute-start.29) | collective-permute-done | bytes 393248 | tf_op jit(solution)/shard_map/ppermute | solution.py:155
  132.3 4.3 %collective-permute-done.31.refs_3_ = bf16[32,48,128]{2,1,0:T(8,128)(2,1)S(1)} collective-permute-done((bf16[32,48,128]{2,1,0:T(8,128)(2,1)S(1)}, bf16[32,48,128]{2,1,0:T(8,128)(2,1)S(1)}, u32[]{:S(2)}, u32[]{:S(2)}) %collective-permute-start.31) | collective-permute-done | bytes 393248 | tf_op jit(solution)/shard_map/ppermute | solution.py:155
  138.0 2.8 %collective-permute-start.32 = (bf16[16,48,128]{2,1,0:T(8,128)(2,1)S(1)}, bf16[16,48,128]{2,1,0:T(8,128)(2,1)S(1)}, u32[]{:S(2)}, u32[]{:S(2)}) collective-permute-start(bf16[16,48,128]{2,1,0:T(8,128)(2,1)S(1)} %get-tuple-element.89), channel_id=1, source_target_pairs={{0,1},{1,2},{2,3},{3,4},{4,5},{5,6},{6,7},{7,0},{8,9},{9,10},{10,1... | collective-permute-start | bytes 589832 | tf_op jit(solution)/shard_map/ppermute | solution.py:212
  143.1 4.7 %collective-permute-done.32.refs_1_ = bf16[16,48,128]{2,1,0:T(8,128)(2,1)S(1)} collective-permute-done((bf16[16,48,128]{2,1,0:T(8,128)(2,1)S(1)}, bf16[16,48,128]{2,1,0:T(8,128)(2,1)S(1)}, u32[]{:S(2)}, u32[]{:S(2)}) %collective-permute-start.32) | collective-permute-done | bytes 196640 | tf_op jit(solution)/shard_map/ppermute | solution.py:212
  151.2 7.2 %collective-permute-done.34.refs_1_ = bf16[16,48,128]{2,1,0:T(8,128)(2,1)S(1)} collective-permute-done((bf16[16,48,128]{2,1,0:T(8,128)(2,1)S(1)}, bf16[16,48,128]{2,1,0:T(8,128)(2,1)S(1)}, u32[]{:S(2)}, u32[]{:S(2)}) %collective-permute-start.34) | collective-permute-done | bytes 196640 | tf_op jit(solution)/shard_map/ppermute | solution.py:212
  162.7 3.6 %collective-permute-done.37.refs_1_ = bf16[16,48,128]{2,1,0:T(8,128)(2,1)S(1)} collective-permute-done((bf16[16,48,128]{2,1,0:T(8,128)(2,1)S(1)}, bf16[16,48,128]{2,1,0:T(8,128)(2,1)S(1)}, u32[]{:S(2)}, u32[]{:S(2)}) %collective-permute-start.37) | collective-permute-done | bytes 196640 | tf_op jit(solution)/shard_map/ppermute | solution.py:212
  166.3 3.0 %collective-permute-start.38 = (bf16[16,48,128]{2,1,0:T(8,128)(2,1)S(1)}, bf16[16,48,128]{2,1,0:T(8,128)(2,1)S(1)}, u32[]{:S(2)}, u32[]{:S(2)}) collective-permute-start(bf16[16,48,128]{2,1,0:T(8,128)(2,1)S(1)} %shard_map.77), channel_id=1, source_target_pairs={{0,7},{1,0},{2,1},{3,2},{4,3},{5,4},{6,5},{7,6},{8,15},{9,8},{10,9... | collective-permute-start | bytes 589832 | tf_op jit(solution)/shard_map/ppermute | solution.py:212
  169.4 5.1 %collective-permute-done.36.refs_5_ = bf16[16,48,128]{2,1,0:T(8,128)(2,1)S(1)} collective-permute-done((bf16[16,48,128]{2,1,0:T(8,128)(2,1)S(1)}, bf16[16,48,128]{2,1,0:T(8,128)(2,1)S(1)}, u32[]{:S(2)}, u32[]{:S(2)}) %collective-permute-start.36) | collective-permute-done | bytes 196640 | tf_op jit(solution)/shard_map/ppermute | solution.py:212
  (111 shorter events, 62.6 us)
Async XLA Ops:
  0.0 38.0 %all-to-all-start = ((bf16[8,32,2048]{2,0,1:T(8,128)(2,1)}), bf16[8,32,2048]{2,0,1:T(8,128)(2,1)S(1)}, u32[]{:S(2)}, u32[]{:S(2)}) async-start(bf16[8,32,2048]{2,0,1:T(8,128)(2,1)} %bitcast.43), calls=%async_computation | async-start | bytes 2097152 | tf_op jit(solution)/shard_map/all_to_all | solution.py:232
  16.1 21.9 %collective-permute-start.5 = (bf16[4,8,256,128]{3,2,1,0:T(8,128)(2,1)}, bf16[4,8,256,128]{3,2,1,0:T(8,128)(2,1)}, u32[]{:S(2)}, u32[]{:S(2)}) collective-permute-start(bf16[4,8,256,128]{3,2,1,0:T(8,128)(2,1)} %get-tuple-element.95), channel_id=1, source_target_pairs={{0,32},{32,0},{64,96},{96,64},{128,160},{160,128},{192,224},{224,1... | collective-permute-start | bytes 6291464 | tf_op jit(solution)/shard_map/ppermute | solution.py:238
  43.8 19.0 %collective-permute-start.13 = (bf16[32,48,128]{2,1,0:T(8,128)(2,1)S(1)}, bf16[32,48,128]{2,1,0:T(8,128)(2,1)S(1)}, u32[]{:S(2)}, u32[]{:S(2)}) collective-permute-start(bf16[32,48,128]{2,1,0:T(8,128)(2,1)S(1)} %get-tuple-element.66), channel_id=1, source_target_pairs={{0,64},{32,96},{64,128},{96,160},{128,192},{160,224},{192,0},{224,... | collective-permute-start | bytes 1179656 | tf_op jit(solution)/shard_map/ppermute | solution.py:155
  45.3 17.4 %collective-permute-start.14 = (bf16[32,48,128]{2,1,0:T(8,128)(2,1)S(1)}, bf16[32,48,128]{2,1,0:T(8,128)(2,1)S(1)}, u32[]{:S(2)}, u32[]{:S(2)}) collective-permute-start(bf16[32,48,128]{2,1,0:T(8,128)(2,1)S(1)} %get-tuple-element.67), channel_id=1, source_target_pairs={{0,128},{32,160},{64,192},{96,224},{128,0},{160,32},{192,64},{224,... | collective-permute-start | bytes 1179656 | tf_op jit(solution)/shard_map/ppermute | solution.py:155
  46.4 20.9 %collective-permute-start.15 = (bf16[32,48,128]{2,1,0:T(8,128)(2,1)S(1)}, bf16[32,48,128]{2,1,0:T(8,128)(2,1)S(1)}, u32[]{:S(2)}, u32[]{:S(2)}) collective-permute-start(bf16[32,48,128]{2,1,0:T(8,128)(2,1)S(1)} %get-tuple-element.68), channel_id=1, source_target_pairs={{0,192},{32,224},{64,0},{96,32},{128,64},{160,96},{192,128},{224,1... | collective-permute-start | bytes 1179656 | tf_op jit(solution)/shard_map/ppermute | solution.py:155
  51.0 18.9 %collective-permute-start.7 = (bf16[32,32,128]{2,1,0:T(8,128)(2,1)S(1)}, bf16[32,32,128]{2,1,0:T(8,128)(2,1)S(1)}, u32[]{:S(2)}, u32[]{:S(2)}) collective-permute-start(bf16[32,32,128]{2,1,0:T(8,128)(2,1)S(1)} %get-tuple-element.58), channel_id=1, source_target_pairs={{0,64},{32,96},{64,128},{96,160},{128,192},{160,224},{192,0},{224,... | collective-permute-start | bytes 786440 | tf_op jit(solution)/shard_map/ppermute | solution.py:155
  51.1 21.8 %collective-permute-start.8 = (bf16[32,32,128]{2,1,0:T(8,128)(2,1)S(1)}, bf16[32,32,128]{2,1,0:T(8,128)(2,1)S(1)}, u32[]{:S(2)}, u32[]{:S(2)}) collective-permute-start(bf16[32,32,128]{2,1,0:T(8,128)(2,1)S(1)} %get-tuple-element.59), channel_id=1, source_target_pairs={{0,128},{32,160},{64,192},{96,224},{128,0},{160,32},{192,64},{224,... | collective-permute-start | bytes 786440 | tf_op jit(solution)/shard_map/ppermute | solution.py:155
  62.8 13.9 %collective-permute-start.9 = (bf16[32,32,128]{2,1,0:T(8,128)(2,1)S(1)}, bf16[32,32,128]{2,1,0:T(8,128)(2,1)S(1)}, u32[]{:S(2)}, u32[]{:S(2)}) collective-permute-start(bf16[32,32,128]{2,1,0:T(8,128)(2,1)S(1)} %get-tuple-element.60), channel_id=1, source_target_pairs={{0,192},{32,224},{64,0},{96,32},{128,64},{160,96},{192,128},{224,1... | collective-permute-start | bytes 786440 | tf_op jit(solution)/shard_map/ppermute | solution.py:155
  68.2 37.7 %collective-permute-start.16 = (bf16[32,48,128]{2,1,0:T(8,128)(2,1)S(1)}, bf16[32,48,128]{2,1,0:T(8,128)(2,1)S(1)}, u32[]{:S(2)}, u32[]{:S(2)}) collective-permute-start(bf16[32,48,128]{2,1,0:T(8,128)(2,1)S(1)} %get-tuple-element.70), channel_id=1, source_target_pairs={{0,8},{1,9},{2,10},{3,11},{4,12},{5,13},{6,14},{7,15},{8,16},{9,17... | collective-permute-start | bytes 1179656 | tf_op jit(solution)/shard_map/ppermute | solution.py:155
  79.1 24.1 %collective-permute-start.11 = (bf16[32,32,128]{2,1,0:T(8,128)(2,1)S(1)}, bf16[32,32,128]{2,1,0:T(8,128)(2,1)S(1)}, u32[]{:S(2)}, u32[]{:S(2)}) collective-permute-start(bf16[32,32,128]{2,1,0:T(8,128)(2,1)S(1)} %get-tuple-element.63), channel_id=1, source_target_pairs={{0,16},{1,17},{2,18},{3,19},{4,20},{5,21},{6,22},{7,23},{8,24},{9,... | collective-permute-start | bytes 786440 | tf_op jit(solution)/shard_map/ppermute | solution.py:155
  82.4 21.8 %collective-permute-start.12 = (bf16[32,32,128]{2,1,0:T(8,128)(2,1)S(1)}, bf16[32,32,128]{2,1,0:T(8,128)(2,1)S(1)}, u32[]{:S(2)}, u32[]{:S(2)}) collective-permute-start(bf16[32,32,128]{2,1,0:T(8,128)(2,1)S(1)} %get-tuple-element.64), channel_id=1, source_target_pairs={{0,24},{1,25},{2,26},{3,27},{4,28},{5,29},{6,30},{7,31},{8,0},{9,1... | collective-permute-start | bytes 786440 | tf_op jit(solution)/shard_map/ppermute | solution.py:155
  82.6 26.9 %collective-permute-start.17 = (bf16[32,48,128]{2,1,0:T(8,128)(2,1)S(1)}, bf16[32,48,128]{2,1,0:T(8,128)(2,1)S(1)}, u32[]{:S(2)}, u32[]{:S(2)}) collective-permute-start(bf16[32,48,128]{2,1,0:T(8,128)(2,1)S(1)} %get-tuple-element.71), channel_id=1, source_target_pairs={{0,16},{1,17},{2,18},{3,19},{4,20},{5,21},{6,22},{7,23},{8,24},{9,... | collective-permute-start | bytes 1179656 | tf_op jit(solution)/shard_map/ppermute | solution.py:155
  87.5 22.9 %collective-permute-start.18 = (bf16[32,48,128]{2,1,0:T(8,128)(2,1)S(1)}, bf16[32,48,128]{2,1,0:T(8,128)(2,1)S(1)}, u32[]{:S(2)}, u32[]{:S(2)}) collective-permute-start(bf16[32,48,128]{2,1,0:T(8,128)(2,1)S(1)} %get-tuple-element.72), channel_id=1, source_target_pairs={{0,24},{1,25},{2,26},{3,27},{4,28},{5,29},{6,30},{7,31},{8,0},{9,1... | collective-permute-start | bytes 1179656 | tf_op jit(solution)/shard_map/ppermute | solution.py:155
  103.2 12.1 %collective-permute-start.26 = (bf16[32,48,128]{2,1,0:T(8,128)(2,1)S(1)}, bf16[32,48,128]{2,1,0:T(8,128)(2,1)S(1)}, u32[]{:S(2)}, u32[]{:S(2)}) collective-permute-start(bf16[32,48,128]{2,1,0:T(8,128)(2,1)S(1)} %get-tuple-element.81), channel_id=1, source_target_pairs={{0,64},{32,96},{64,128},{96,160},{128,192},{160,224},{192,0},{224,... | collective-permute-start | bytes 1179656 | tf_op jit(solution)/shard_map/ppermute | solution.py:155
  105.9 11.8 %collective-permute-start.28 = (bf16[32,48,128]{2,1,0:T(8,128)(2,1)S(1)}, bf16[32,48,128]{2,1,0:T(8,128)(2,1)S(1)}, u32[]{:S(2)}, u32[]{:S(2)}) collective-permute-start(bf16[32,48,128]{2,1,0:T(8,128)(2,1)S(1)} %get-tuple-element.83), channel_id=1, source_target_pairs={{0,192},{32,224},{64,0},{96,32},{128,64},{160,96},{192,128},{224,1... | collective-permute-start | bytes 1179656 | tf_op jit(solution)/shard_map/ppermute | solution.py:155
  118.6 12.1 %collective-permute-start.29 = (bf16[32,48,128]{2,1,0:T(8,128)(2,1)S(1)}, bf16[32,48,128]{2,1,0:T(8,128)(2,1)S(1)}, u32[]{:S(2)}, u32[]{:S(2)}) collective-permute-start(bf16[32,48,128]{2,1,0:T(8,128)(2,1)S(1)} %get-tuple-element.85), channel_id=1, source_target_pairs={{0,8},{1,9},{2,10},{3,11},{4,12},{5,13},{6,14},{7,15},{8,16},{9,17... | collective-permute-start | bytes 1179656 | tf_op jit(solution)/shard_map/ppermute | solution.py:155
  118.7 13.6 %collective-permute-start.30 = (bf16[32,48,128]{2,1,0:T(8,128)(2,1)S(1)}, bf16[32,48,128]{2,1,0:T(8,128)(2,1)S(1)}, u32[]{:S(2)}, u32[]{:S(2)}) collective-permute-start(bf16[32,48,128]{2,1,0:T(8,128)(2,1)S(1)} %get-tuple-element.86), channel_id=1, source_target_pairs={{0,16},{1,17},{2,18},{3,19},{4,20},{5,21},{6,22},{7,23},{8,24},{9,... | collective-permute-start | bytes 1179656 | tf_op jit(solution)/shard_map/ppermute | solution.py:155
  120.8 15.9 %collective-permute-start.31 = (bf16[32,48,128]{2,1,0:T(8,128)(2,1)S(1)}, bf16[32,48,128]{2,1,0:T(8,128)(2,1)S(1)}, u32[]{:S(2)}, u32[]{:S(2)}) collective-permute-start(bf16[32,48,128]{2,1,0:T(8,128)(2,1)S(1)} %get-tuple-element.87), channel_id=1, source_target_pairs={{0,24},{1,25},{2,26},{3,27},{4,28},{5,29},{6,30},{7,31},{8,0},{9,1... | collective-permute-start | bytes 1179656 | tf_op jit(solution)/shard_map/ppermute | solution.py:155
  123.8 18.3 %collective-permute-start.21 = (bf16[16,80,128]{2,1,0:T(8,128)(2,1)S(1)}, bf16[16,80,128]{2,1,0:T(8,128)(2,1)S(1)}, u32[]{:S(2)}, u32[]{:S(2)}) collective-permute-start(bf16[16,80,128]{2,1,0:T(8,128)(2,1)S(1)} %get-tuple-element.76), channel_id=1, source_target_pairs={{0,1},{1,2},{2,3},{3,4},{4,5},{5,6},{6,7},{7,0},{8,9},{9,10},{10,1... | collective-permute-start | bytes 983048 | tf_op jit(solution)/shard_map/ppermute | solution.py:212
  125.0 17.1 %collective-permute-start.22 = (bf16[16,80,128]{2,1,0:T(8,128)(2,1)S(1)}, bf16[16,80,128]{2,1,0:T(8,128)(2,1)S(1)}, u32[]{:S(2)}, u32[]{:S(2)}) collective-permute-start(bf16[16,80,128]{2,1,0:T(8,128)(2,1)S(1)} %get-tuple-element.77), channel_id=1, source_target_pairs={{0,7},{1,0},{2,1},{3,2},{4,3},{5,4},{6,5},{7,6},{8,15},{9,8},{10,9... | collective-permute-start | bytes 983048 | tf_op jit(solution)/shard_map/ppermute | solution.py:212
  142.3 18.1 %collective-permute-start.23 = (bf16[16,80,128]{2,1,0:T(8,128)(2,1)S(1)}, bf16[16,80,128]{2,1,0:T(8,128)(2,1)S(1)}, u32[]{:S(2)}, u32[]{:S(2)}) collective-permute-start(bf16[16,80,128]{2,1,0:T(8,128)(2,1)S(1)} %get-tuple-element.78), channel_id=1, source_target_pairs={{0,1},{1,2},{2,3},{3,4},{4,5},{5,6},{6,7},{7,0},{8,9},{9,10},{10,1... | collective-permute-start | bytes 983048 | tf_op jit(solution)/shard_map/ppermute | solution.py:212
  160.3 15.7 %collective-permute-start.25 = (bf16[16,80,128]{2,1,0:T(8,128)(2,1)S(1)}, bf16[16,80,128]{2,1,0:T(8,128)(2,1)S(1)}, u32[]{:S(2)}, u32[]{:S(2)}) collective-permute-start(bf16[16,80,128]{2,1,0:T(8,128)(2,1)S(1)} %get-tuple-element.79), channel_id=1, source_target_pairs={{0,7},{1,0},{2,1},{3,2},{4,3},{5,4},{6,5},{7,6},{8,15},{9,8},{10,9... | collective-permute-start | bytes 983048 | tf_op jit(solution)/shard_map/ppermute | solution.py:212
  160.4 15.6 %collective-permute-start.24 = (bf16[16,80,128]{2,1,0:T(8,128)(2,1)S(1)}, bf16[16,80,128]{2,1,0:T(8,128)(2,1)S(1)}, u32[]{:S(2)}, u32[]{:S(2)}) collective-permute-start(bf16[16,80,128]{2,1,0:T(8,128)(2,1)S(1)} %shard_map.72), channel_id=1, source_target_pairs={{0,1},{1,2},{2,3},{3,4},{4,5},{5,6},{6,7},{7,0},{8,9},{9,10},{10,1... | collective-permute-start | bytes 983048 | tf_op jit(solution)/shard_map/ppermute | solution.py:212
  162.4 12.0 %collective-permute-start.36 = (bf16[16,48,128]{2,1,0:T(8,128)(2,1)S(1)}, bf16[16,48,128]{2,1,0:T(8,128)(2,1)S(1)}, u32[]{:S(2)}, u32[]{:S(2)}) collective-permute-start(bf16[16,48,128]{2,1,0:T(8,128)(2,1)S(1)} %get-tuple-element.93), channel_id=1, source_target_pairs={{0,1},{1,2},{2,3},{3,4},{4,5},{5,6},{6,7},{7,0},{8,9},{9,10},{10,1... | collective-permute-start | bytes 589832 | tf_op jit(solution)/shard_map/ppermute | solution.py:212
  (20 other events, 193.4 us)
where the time goes:
time: 178 us; the launch traced here: 177 us
  starting transfers between devices  79.5 us (45%)
  waiting for transfers between devices  77.2 us (43%)
  Pallas kernels  14.3 us (8%)
  local copies, waits for them, and re-layouts  4.51 us (3%)
    ppermute x18, starting transfers between devices, exchange(): moved.append(lax.ppermute(parts[k], axis, shift(k)))  39.9 us
    ppermute x18, waiting for transfers between devices, exchange(): moved.append(lax.ppermute(parts[k], axis, shift(k)))  36.7 us
    ppermute x14, waiting for transfers between devices, ring(): part = lax.ppermute(part, 'dev', z_shift(step))  23.9 us
    ppermute x14, starting transfers between devices, ring(): part = lax.ppermute(part, 'dev', z_shift(step))  22.1 us
    pallas_call x15, Pallas kernels, call(): pl.pallas_call(kernel, out_shape=out_shape, in_specs=specs, out_specs=[VM...  14.3 us
    ppermute x5, waiting for transfers between devices, spread(): known = jnp.concatenate([known, lax.ppermute(known, axis, pairs)], axis=0)  12.3 us
    all_to_all x1, starting transfers between devices, body(): lax.all_to_all(residual, 'dev', split_axis=1, concat_axis=0, tiled=True)  11.8 us
    ppermute x5, starting transfers between devices, spread(): known = jnp.concatenate([known, lax.ppermute(known, axis, pairs)], axis=0)  5.13 us
  transfers between devices with their start and end apart: 40, of which 24 were waited for; matrix products, arithmetic and copies ran while one was open for 3% of the time, Pallas kernels for 5%

commit v1 on v0

--- a/solution.py
+++ b/solution.py
@@ -19,14 +19,16 @@
 CHUNKS = (32, 48, 48)
 HOPS = NZ // 2
 VMEM_LIMIT = 10 << 20
-RINGS = ((0, 1), (2,))
+RINGS = ((1,), (2,))
+FOLDS = (0,)
+BITS = 3
 
 
 VMEM = pl.BlockSpec(memory_space=pltpu.VMEM)
 SMEM = pl.BlockSpec(memory_space=pltpu.SMEM)
 
 
-def call(kernel, out_shape, ins, smems, flops=0, scratch=()):
+def call(kernel, out_shape, ins, smems, flops=0, scratch=(), aliases=None):
     specs = [SMEM] * smems + [VMEM] * (len(ins) - smems)
     many = isinstance(out_shape, list)
     return pl.pallas_call(
@@ -35,18 +37,20 @@
         in_specs=specs,
         out_specs=[VMEM] * len(out_shape) if many else VMEM,
         scratch_shapes=list(scratch),
+        input_output_aliases=aliases or {},
         compiler_params=pltpu.CompilerParams(vmem_limit_bytes=VMEM_LIMIT),
         cost_estimate=pl.CostEstimate(flops=flops, bytes_accessed=4 << 20, transcendentals=0),
     )(*ins)
 
 
-def adjoint_kernel(rows, rays_ref, place_ref, own_ref, par_ref, fpo_ref, fpr_ref, *outs):
+def adjoint_kernel(rows, sides, begun, rays_ref, place_ref, *refs):
+    given, outs = refs[: 2 * len(sides)], refs[2 * len(sides) + begun :]
     low, high = rows[0][0], rows[-1][1]
     size = high - low
     blank = jnp.zeros((size, BLK), jnp.bfloat16)
     for k in range(NX):
         to = lax.rem(place_ref[0] + k, NX)
-        for side, (proj, tiles) in enumerate(((own_ref, fpo_ref), (par_ref, fpr_ref))):
+        for side, proj, tiles in zip(sides, given[::2], given[1::2]):
 
             for quad in range(CAP // 4):
                 first = (k * CORES + side) * CAP + quad * 4
@@ -82,7 +86,7 @@
         lax.fori_loop(0, PART // 8, move, 0)
 
 
-def gather_kernel(up_far, earlier, at_ref, *refs):
+def gather_kernel(fars, earlier, at_ref, *refs):
     ins, before, dense = refs[:NY], refs[NY : NY + earlier], refs[NY + earlier]
     sends = refs[NY + earlier + 1 :]
     dense[...] = jnp.zeros_like(dense)
@@ -96,11 +100,11 @@
             return carry
 
         lax.fori_loop(0, PART // 4, add, 0)
-    for send, far in zip(sends, (up_far, up_far + 1)):
+    for send, far in zip(sends, fars):
         low = 0
         for part in tuple(before) + (dense,):
             high = low + part.shape[1]
-            send[:, low:high, :] = part[far * VB : (far + 1) * VB].astype(jnp.bfloat16)
+            send[:, low:high, :] = part[far * VB : far * VB + send.shape[0]].astype(jnp.bfloat16)
             low = high
 
 
@@ -116,10 +120,19 @@
             low = high
 
 
-def finish_kernel(groups, *refs):
+def fold_kernel(keep, came, goes, kept):
+    half = kept.shape[0]
+    kept[...] = keep[:half] + came[:half].astype(jnp.float32)
+    goes[...] = (keep[half : 2 * half] + came[half:].astype(jnp.float32)).astype(jnp.bfloat16)
+
+
+def finish_kernel(folds, groups, *refs):
     parts, out = refs[:-1], refs[-1]
     for b in range(VB):
-        rows, at = [], 0
+        rows = []
+        for i in range(folds):
+            rows.append(parts[2 * i][b] + parts[2 * i + 1][b].astype(jnp.float32))
+        at = 2 * folds
         for group in groups:
             up, down = parts[at + len(group)], parts[at + len(group) + 1]
             low = 0
@@ -149,6 +162,16 @@
     return [(y * NZ + z, y * NZ + (z + k) % NZ) for y in range(NY) for z in range(NZ)]
 
 
+def z_fold(step):
+    size = NX * CORES * NY * NZ
+    pairs = []
+    for i in range(size):
+        g, d = divmod(i, NY * NZ)
+        z, c = d % NZ, g % CORES
+        pairs.append((i, i - z + (((z + c) % NZ ^ (1 << step)) - c) % NZ))
+    return pairs
+
+
 def exchange(parts, axis, shift):
     moved = [parts[0]]
     for k in range(1, len(parts)):
@@ -164,6 +187,10 @@
 
 def flip(size, unit, bit):
     return [(i, i ^ (bit * unit)) for i in range(size)]
+
+
+def turned(e):
+    return (e & 1) * 4 + (e & 2) + e // 4
 
 
 def routes(slot_ray, slot_vox, slot_count, x, c, y, z):
@@ -190,12 +217,14 @@
     target = turn * PART + jnp.sum(same.astype(jnp.int32), axis=2)
     hit = (target[:, None, :] == slots[None, :, None]).astype(jnp.int32)
     src = jnp.sum(hit[0] * slots[None, :], axis=1)
-    place = lax.rem(lax.rem(vox // VB, NZ) - z + NZ, NZ) * VB + lax.rem(vox, VB)
-    at = jnp.sum(hit * place[:, None, :], axis=2).reshape(NY, NY, PART)
+    near_z = lax.rem(lax.rem(vox // VB, NZ) - z + NZ, NZ)
+    fold_z = turned(jnp.bitwise_xor(lax.rem(lax.rem(vox // VB, NZ) + c, NZ), lax.rem(z + c, NZ)))
     entry = jnp.bitwise_xor(y, lax.rem(y - jnp.arange(NY, dtype=jnp.int32) + NY, NY))
     pick = (entry[:, None] == jnp.arange(NY, dtype=jnp.int32)[None, :]).astype(jnp.int32)
-    at = jnp.sum(pick[:, :, None] * jnp.transpose(at, (1, 0, 2)), axis=1).reshape(NY * PART)
-    return rays, src, at
+    both = (near_z * VB + lax.rem(vox, VB)) * (NZ * VB) + fold_z * VB + lax.rem(vox, VB)
+    both = jnp.sum(hit * both[:, None, :], axis=2).reshape(NY, NY, PART)
+    both = jnp.sum(pick[:, :, None] * jnp.transpose(both, (1, 0, 2)), axis=1).reshape(NY * PART)
+    return rays, src, both // (NZ * VB), lax.rem(both, NZ * VB)
 
 
 def turns(r):
@@ -203,27 +232,25 @@
     return list(range(up_far, 0, -1)), list(range(up_far + 1, NZ))
 
 
+def ways(r):
+    return sorted(zip(("up", "down"), turns(r)), key=lambda way: -len(way[1]))
+
+
 def ring(r, dense, up, down):
-    ups, downs = turns(r)
-    for hop in range(HOPS):
-        sent = []
-        for part, far, step in ((up, ups, 1), (down, downs, NZ - 1)):
-            if hop < len(far):
-                part = lax.ppermute(part, "dev", z_shift(step))
-            sent.append(part)
-        up, down = sent
-        places = [far[hop + 1] for far in (ups, downs) if hop + 1 < len(far)]
-        if places:
-            going = [part for part, far in ((up, ups), (down, downs)) if hop + 1 < len(far)]
-            going = call(
-                functools.partial(hop_kernel, places, len(dense)),
-                [pltpu.VMEM(part.shape, part.dtype) for part in going],
-                dense + going,
-                0,
-            )
-            up = going[0] if hop + 1 < len(ups) else up
-            down = going[-1] if hop + 1 < len(downs) else down
-    return dense + [up, down]
+    ends = dict(up=up, down=down)
+    for way, far in ways(r):
+        part = ends[way]
+        for hop in range(len(far)):
+            part = lax.ppermute(part, "dev", z_shift(1 if way == "up" else NZ - 1))
+            if hop + 1 < len(far):
+                (part,) = call(
+                    functools.partial(hop_kernel, far[hop + 1 : hop + 2], len(dense)),
+                    [pltpu.VMEM(part.shape, part.dtype)],
+                    dense + [part],
+                    0,
+                )
+        ends[way] = part
+    return dense + [ends["up"], ends["down"]]
 
 
 def body(residual, coefficients, slot_ray, slot_vox, slot_count, footprint):
@@ -236,44 +263,77 @@
     fpo = lax.dynamic_index_in_dim(tiles, c, 1, keepdims=False)
     fpr = lax.dynamic_index_in_dim(tiles, 1 - c, 1, keepdims=False)
     fpr = lax.ppermute(fpr, "grp", core_swap())
-    panel, (rays, src, at), place, fpo, fpr = lax.optimization_barrier((panel, tables, place, fpo, fpr))
+    panel, (rays, src, at, at_fold), place, fpo, fpr = lax.optimization_barrier((panel, tables, place, fpo, fpr))
     own = lax.dot_general(
         coefficients, panel, (((0,), (0,)), ((), ())), preferred_element_type=jnp.float32
     ).astype(jnp.bfloat16)
     par = lax.ppermute(own, "grp", core_swap())
     rows = [(sum(CHUNKS[:i]), sum(CHUNKS[: i + 1])) for i in range(len(CHUNKS))]
     made = []
-    for some in (rows[:1], rows[1:]):
-        made += call(
-            functools.partial(adjoint_kernel, some),
+    for name, some, sides in (("adjo", rows[:1], (0,)), ("adj0", rows[:1], (1,)), ("adj1", rows[1:], (0, 1))):
+        begun = made if name == "adj0" else []
+        ins = [rays, place]
+        for side in sides:
+            ins += [(own, par)[side], (fpo, fpr)[side]]
+        parts = call(
+            functools.partial(adjoint_kernel, some, sides, len(begun)),
             [pltpu.VMEM((PART, hi - lo, BLK), jnp.bfloat16) for lo, hi in some for _ in range(NX)],
-            [rays, place, own, par, fpo, fpr],
+            ins + list(begun),
             2,
+            aliases={len(ins) + j: j for j in range(len(begun))},
         )
+        made = list(parts) if name != "adj1" else made + list(parts)
+
+    def arrive(i):
+        block = pltpu.VMEM((PART, CHUNKS[i], BLK), jnp.bfloat16)
+        parts = exchange(made[i * NX : (i + 1) * NX], "grp", x_shift)
+        parts = call(
+            pack_kernel, [block] * NY, [src] + parts, 1, scratch=[pltpu.VMEM((NX * PART, CHUNKS[i], BLK), jnp.bfloat16)]
+        )
+        return exchange(parts, "dev", y_shift)
+
     ends = []
+    for i in FOLDS:
+        parts = arrive(i)
+        half = NZ * VB // 2
+        tail = (CHUNKS[i], BLK)
+        keep, part = call(
+            functools.partial(gather_kernel, (NZ // 2,), 0),
+            [pltpu.VMEM((NZ * VB,) + tail, jnp.float32), pltpu.VMEM((half,) + tail, jnp.bfloat16)],
+            [at_fold] + parts,
+            1,
+        )
+        for step in range(BITS):
+            part = lax.ppermute(part, ("grp", "dev"), z_fold(step))
+            if step < BITS - 1:
+                half //= 2
+                part, keep = call(
+                    fold_kernel,
+                    [pltpu.VMEM((half,) + tail, jnp.bfloat16), pltpu.VMEM((half,) + tail, jnp.float32)],
+                    [keep, part],
+                    0,
+                )
+        ends += [keep, part]
     for r, group in enumerate(RINGS):
         dense = []
         for i in group:
-            size = CHUNKS[i]
-            block = pltpu.VMEM((PART, size, BLK), jnp.bfloat16)
-            parts = exchange(made[i * NX : (i + 1) * NX], "grp", x_shift)
-            parts = call(
-                pack_kernel, [block] * NY, [src] + parts, 1, scratch=[pltpu.VMEM((NX * PART, size, BLK), jnp.bfloat16)]
-            )
-            parts = exchange(parts, "dev", y_shift)
+            parts = arrive(i)
             sends = []
             if i == group[-1]:
                 sends = [pltpu.VMEM((VB, sum(CHUNKS[j] for j in group), BLK), jnp.bfloat16)] * 2
             before = dense if sends else []
+            far = turns(r)[0][0]
             came = call(
-                functools.partial(gather_kernel, turns(r)[0][0], len(before)),
-                [pltpu.VMEM((NZ * VB, size, BLK), jnp.float32)] + sends,
+                functools.partial(gather_kernel, (far, far + 1), len(before)),
+                [pltpu.VMEM((NZ * VB, CHUNKS[i], BLK), jnp.float32)] + sends,
                 [at] + parts + before,
                 1,
             )
             dense = dense + [came[0]]
         ends += ring(r, dense, came[1], came[2])
-    return call(functools.partial(finish_kernel, RINGS), jax.ShapeDtypeStruct((VB * BLK, BLK), jnp.float32), ends, 0)
+    return call(
+        functools.partial(finish_kernel, len(FOLDS), RINGS), jax.ShapeDtypeStruct((VB * BLK, BLK), jnp.float32), ends, 0
+    )
 
 
 def solution(mesh):

time: 178 us -> 196 us (1.10)
  the two profiles are of different devices: /device:TPU:10 before, /device:TPU:8 now
where the time goes in v1:
time: 196 us
  starting transfers between devices  89.9 us (46%)
  waiting for transfers between devices  84.9 us (43%)
  Pallas kernels  15 us (8%)
  local copies, waits for them, and re-layouts  4.49 us (2%)
    ppermute x18, waiting for transfers between devices, exchange(): moved.append(lax.ppermute(parts[k], axis, shift(k)))  49.9 us
    ppermute x18, starting transfers between devices, exchange(): moved.append(lax.ppermute(parts[k], axis, shift(k)))  40.5 us
    ppermute x14, starting transfers between devices, ring(): part = lax.ppermute(part, 'dev', z_shift(1 if way == 'up' else NZ - 1))  23.9 us
    pallas_call x22, Pallas kernels, call(): pl.pallas_call(kernel, out_shape=out_shape, in_specs=specs, out_specs=[VM...  15 us
    ppermute x14, waiting for transfers between devices, ring(): part = lax.ppermute(part, 'dev', z_shift(1 if way == 'up' else NZ - 1))  12.7 us
    all_to_all x1, starting transfers between devices, body(): lax.all_to_all(residual, 'dev', split_axis=1, concat_axis=0, tiled=True)  11.8 us
    ppermute x5, waiting for transfers between devices, spread(): known = jnp.concatenate([known, lax.ppermute(known, axis, pairs)], axis=0)  10.5 us
    ppermute x3, waiting for transfers between devices, body(): part = lax.ppermute(part, ('grp', 'dev'), z_fold(step))  7.6 us
  transfers between devices with their start and end apart: 43, of which 18 were waited for; matrix products, arithmetic and copies ran while one was open for 3% of the time, Pallas kernels for 5%

profile of v1, /device:TPU:8, one launch (start us, length us, event | category | flops | bytes accessed | tf_op | source)
XLA Modules:
  0.0 196.2 jit_solution(13562032549352263858)
XLA Ops:
  0.0 11.8 %all-to-all-start = ((bf16[8,32,2048]{2,0,1:T(8,128)(2,1)}), bf16[8,32,2048]{2,0,1:T(8,128)(2,1)S(1)}, u32[]{:S(2)}, u32[]{:S(2)}) async-start(bf16[8,32,2048]{2,0,1:T(8,128)(2,1)} %bitcast.43), calls=%async_computation | async-start | bytes 2097152 | tf_op jit(solution)/shard_map/all_to_all | solution.py:259
  12.1 4.0 %dynamic-slice_bitcast_fusion = (bf16[4,8,256,128]{3,2,1,0:T(8,128)(2,1)}, bf16[4,8,256,128]{3,2,1,0:T(8,128)(2,1)S(1)}) fusion(bf16[4,2,8,256,128]{4,3,2,1,0:T(8,128)(2,1)} %bitcast.41, s32[]{:T(128)S(6)} %select_n.92, s32[]{:T(128)S(6)} %select_n.80), kind=kLoop, calls=%fused_computation.2 | loop fusion | bytes 8388616 | tf_op jit(solution)/shard_map/jit(dynamic_index_in_dim)/squeeze | solution.py:264
  20.4 3.0 %collective-permute-start.2 = (s32[4,8,32]{2,1,0:T(8,128)S(1)}, s32[4,8,32]{2,1,0:T(8,128)S(1)}, u32[]{:S(2)}, u32[]{:S(2)}) collective-permute-start(s32[4,8,32]{2,1,0:T(8,128)S(1)} %pad_add_fusion.1), channel_id=1, source_target_pairs={{0,128},{32,160},{64,192},{96,224},{128,0},{160,32},{192,64},{224,... | collective-permute-start | bytes 12296 | tf_op jit(solution)/shard_map/ppermute | solution.py:184
  26.3 3.3 %collective-permute-done.3 = s32[1,128]{1,0:T(1,128)S(1)} collective-permute-done((s32[1,128]{1,0:T(1,128)S(1)}, s32[1,128]{1,0:T(1,128)S(1)}, u32[]{:S(2)}, u32[]{:S(2)}) %collective-permute-start.3) | collective-permute-done | bytes 544 | tf_op jit(solution)/shard_map/ppermute | solution.py:184
  31.8 2.9 %collective-permute-done.4 = s32[2,128]{1,0:T(2,128)S(1)} collective-permute-done((s32[2,128]{1,0:T(2,128)S(1)}, s32[2,128]{1,0:T(2,128)S(1)}, u32[]{:S(2)}, u32[]{:S(2)}) %collective-permute-start.4) | collective-permute-done | bytes 1056 | tf_op jit(solution)/shard_map/ppermute | solution.py:184
  40.3 3.4 %shard_map.70 = (bf16[32,48,128]{2,1,0:T(8,128)(2,1)S(1)}, bf16[32,48,128]{2,1,0:T(8,128)(2,1)S(1)}, bf16[32,48,128]{2,1,0:T(8,128)(2,1)S(1)}, bf16[32,48,128]{2...) custom-call(s32[128]{0:T(128)S(1)} %reshape.507.rays_ref, ...), custom_call_target="tpu_custom_call" | custom-call | bytes 4194304 | tf_op jit(solution)/shard_map/pallas_call | solution.py:34
  45.3 2.7 %collective-permute-start.17 = (bf16[32,48,128]{2,1,0:T(8,128)(2,1)S(1)}, bf16[32,48,128]{2,1,0:T(8,128)(2,1)S(1)}, u32[]{:S(2)}, u32[]{:S(2)}) collective-permute-start(bf16[32,48,128]{2,1,0:T(8,128)(2,1)S(1)} %get-tuple-element.81), channel_id=1, source_target_pairs={{0,128},{32,160},{64,192},{96,224},{128,0},{160,32},{192,64},{224,... | collective-permute-start | bytes 1179656 | tf_op jit(solution)/shard_map/ppermute | solution.py:178
  51.3 3.2 %collective-permute-start.18 = (bf16[32,48,128]{2,1,0:T(8,128)(2,1)S(1)}, bf16[32,48,128]{2,1,0:T(8,128)(2,1)S(1)}, u32[]{:S(2)}, u32[]{:S(2)}) collective-permute-start(bf16[32,48,128]{2,1,0:T(8,128)(2,1)S(1)} %get-tuple-element.82), channel_id=1, source_target_pairs={{0,192},{32,224},{64,0},{96,32},{128,64},{160,96},{192,128},{224,1... | collective-permute-start | bytes 1179656 | tf_op jit(solution)/shard_map/ppermute | solution.py:178
  54.5 16.5 %collective-permute-done.7.refs_1_ = bf16[32,32,128]{2,1,0:T(8,128)(2,1)S(1)} collective-permute-done((bf16[32,32,128]{2,1,0:T(8,128)(2,1)S(1)}, bf16[32,32,128]{2,1,0:T(8,128)(2,1)S(1)}, u32[]{:S(2)}, u32[]{:S(2)}) %collective-permute-start.7) | collective-permute-done | bytes 262176 | tf_op jit(solution)/shard_map/ppermute | solution.py:178
  77.9 15.9 %collective-permute-done.8.refs_2_ = bf16[32,32,128]{2,1,0:T(8,128)(2,1)S(1)} collective-permute-done((bf16[32,32,128]{2,1,0:T(8,128)(2,1)S(1)}, bf16[32,32,128]{2,1,0:T(8,128)(2,1)S(1)}, u32[]{:S(2)}, u32[]{:S(2)}) %collective-permute-start.8) | collective-permute-done | bytes 262176 | tf_op jit(solution)/shard_map/ppermute | solution.py:178
  97.6 2.9 %collective-permute-start.11 = (bf16[32,32,128]{2,1,0:T(8,128)(2,1)S(1)}, bf16[32,32,128]{2,1,0:T(8,128)(2,1)S(1)}, u32[]{:S(2)}, u32[]{:S(2)}) collective-permute-start(bf16[32,32,128]{2,1,0:T(8,128)(2,1)S(1)} %get-tuple-element.70), channel_id=1, source_target_pairs={{0,16},{1,17},{2,18},{3,19},{4,20},{5,21},{6,22},{7,23},{8,24},{9,... | collective-permute-start | bytes 786440 | tf_op jit(solution)/shard_map/ppermute | solution.py:178
  103.9 8.1 %collective-permute-done.10.refs_1_ = bf16[32,32,128]{2,1,0:T(8,128)(2,1)S(1)} collective-permute-done((bf16[32,32,128]{2,1,0:T(8,128)(2,1)S(1)}, bf16[32,32,128]{2,1,0:T(8,128)(2,1)S(1)}, u32[]{:S(2)}, u32[]{:S(2)}) %collective-permute-start.10) | collective-permute-done | bytes 262176 | tf_op jit(solution)/shard_map/ppermute | solution.py:178
  112.1 16.5 %collective-permute-start.21 = (bf16[32,48,128]{2,1,0:T(8,128)(2,1)S(1)}, bf16[32,48,128]{2,1,0:T(8,128)(2,1)S(1)}, u32[]{:S(2)}, u32[]{:S(2)}) collective-permute-start(bf16[32,48,128]{2,1,0:T(8,128)(2,1)S(1)} %get-tuple-element.86), channel_id=1, source_target_pairs={{0,24},{1,25},{2,26},{3,27},{4,28},{5,29},{6,30},{7,31},{8,0},{9,1... | collective-permute-start | bytes 1179656 | tf_op jit(solution)/shard_map/ppermute | solution.py:178
  132.6 2.7 %collective-permute-done.21.refs_3_ = bf16[32,48,128]{2,1,0:T(8,128)(2,1)S(1)} collective-permute-done((bf16[32,48,128]{2,1,0:T(8,128)(2,1)S(1)}, bf16[32,48,128]{2,1,0:T(8,128)(2,1)S(1)}, u32[]{:S(2)}, u32[]{:S(2)}) %collective-permute-start.21) | collective-permute-done | bytes 393248 | tf_op jit(solution)/shard_map/ppermute | solution.py:178
  138.8 2.6 %collective-permute-done.33.refs_2_ = bf16[32,48,128]{2,1,0:T(8,128)(2,1)S(1)} collective-permute-done((bf16[32,48,128]{2,1,0:T(8,128)(2,1)S(1)}, bf16[32,48,128]{2,1,0:T(8,128)(2,1)S(1)}, u32[]{:S(2)}, u32[]{:S(2)}) %collective-permute-start.33) | collective-permute-done | bytes 393248 | tf_op jit(solution)/shard_map/ppermute | solution.py:178
  141.4 4.0 %collective-permute-done.34.refs_3_ = bf16[32,48,128]{2,1,0:T(8,128)(2,1)S(1)} collective-permute-done((bf16[32,48,128]{2,1,0:T(8,128)(2,1)S(1)}, bf16[32,48,128]{2,1,0:T(8,128)(2,1)S(1)}, u32[]{:S(2)}, u32[]{:S(2)}) %collective-permute-start.34) | collective-permute-done | bytes 393248 | tf_op jit(solution)/shard_map/ppermute | solution.py:178
  151.4 3.3 %collective-permute-done.38.refs_1_ = bf16[16,48,128]{2,1,0:T(8,128)(2,1)S(1)} collective-permute-done((bf16[16,48,128]{2,1,0:T(8,128)(2,1)S(1)}, bf16[16,48,128]{2,1,0:T(8,128)(2,1)S(1)}, u32[]{:S(2)}, u32[]{:S(2)}) %collective-permute-start.38) | collective-permute-done | bytes 196640 | tf_op jit(solution)/shard_map/ppermute | solution.py:244
  154.8 3.0 %collective-permute-start.39 = (bf16[16,48,128]{2,1,0:T(8,128)(2,1)S(1)}, bf16[16,48,128]{2,1,0:T(8,128)(2,1)S(1)}, u32[]{:S(2)}, u32[]{:S(2)}) collective-permute-start(bf16[16,48,128]{2,1,0:T(8,128)(2,1)S(1)} %shard_map.82), channel_id=1, source_target_pairs={{0,7},{1,0},{2,1},{3,2},{4,3},{5,4},{6,5},{7,6},{8,15},{9,8},{10,9... | collective-permute-start | bytes 589832 | tf_op jit(solution)/shard_map/ppermute | solution.py:244
  159.0 3.0 %collective-permute-start.27 = (bf16[16,48,128]{2,1,0:T(8,128)(2,1)S(1)}, bf16[16,48,128]{2,1,0:T(8,128)(2,1)S(1)}, u32[]{:S(2)}, u32[]{:S(2)}) collective-permute-start(bf16[16,48,128]{2,1,0:T(8,128)(2,1)S(1)} %shard_map.76), channel_id=1, source_target_pairs={{0,7},{1,0},{2,1},{3,2},{4,3},{5,4},{6,5},{7,6},{8,15},{9,8},{10,9... | collective-permute-start | bytes 589832 | tf_op jit(solution)/shard_map/ppermute | solution.py:244
  163.9 3.3 %collective-permute-start.24 = (bf16[16,48,128]{2,1,0:T(8,128)(2,1)S(1)}, bf16[16,48,128]{2,1,0:T(8,128)(2,1)S(1)}, u32[]{:S(2)}, u32[]{:S(2)}) collective-permute-start(bf16[16,48,128]{2,1,0:T(8,128)(2,1)S(1)} %shard_map.74), channel_id=1, source_target_pairs={{0,1},{1,2},{2,3},{3,4},{4,5},{5,6},{6,7},{7,0},{8,9},{9,10},{10,1... | collective-permute-start | bytes 589832 | tf_op jit(solution)/shard_map/ppermute | solution.py:244
  167.9 2.8 %collective-permute-start.28 = (bf16[16,48,128]{2,1,0:T(8,128)(2,1)S(1)}, bf16[16,48,128]{2,1,0:T(8,128)(2,1)S(1)}, u32[]{:S(2)}, u32[]{:S(2)}) collective-permute-start(bf16[16,48,128]{2,1,0:T(8,128)(2,1)S(1)} %shard_map.77), channel_id=1, source_target_pairs={{0,7},{1,0},{2,1},{3,2},{4,3},{5,4},{6,5},{7,6},{8,15},{9,8},{10,9... | collective-permute-start | bytes 589832 | tf_op jit(solution)/shard_map/ppermute | solution.py:244
  172.8 7.2 %collective-permute-done.24.refs_1_ = bf16[16,48,128]{2,1,0:T(8,128)(2,1)S(1)} collective-permute-done((bf16[16,48,128]{2,1,0:T(8,128)(2,1)S(1)}, bf16[16,48,128]{2,1,0:T(8,128)(2,1)S(1)}, u32[]{:S(2)}, u32[]{:S(2)}) %collective-permute-start.24) | collective-permute-done | bytes 196640 | tf_op jit(solution)/shard_map/ppermute | solution.py:244
  183.5 3.7 %collective-permute-start.15 = (bf16[16,32,128]{2,1,0:T(8,128)(2,1)S(1)}, bf16[16,32,128]{2,1,0:T(8,128)(2,1)S(1)}, u32[]{:S(2)}, u32[]{:S(2)}) collective-permute-start(bf16[16,32,128]{2,1,0:T(8,128)(2,1)S(1)} %get-tuple-element.77), channel_id=1, source_target_pairs={{0,4},{1,5},{2,6},{3,7},{4,0},{5,1},{6,2},{7,3},{8,12},{9,13},{10,... | collective-permute-start | bytes 393224 | tf_op jit(solution)/shard_map/ppermute | solution.py:307
  187.3 7.6 %collective-permute-done.15.refs_1_ = bf16[16,32,128]{2,1,0:T(8,128)(2,1)S(1)} collective-permute-done((bf16[16,32,128]{2,1,0:T(8,128)(2,1)S(1)}, bf16[16,32,128]{2,1,0:T(8,128)(2,1)S(1)}, u32[]{:S(2)}, u32[]{:S(2)}) %collective-permute-start.15) | collective-permute-done | bytes 131104 | tf_op jit(solution)/shard_map/ppermute | solution.py:307
  (125 shorter events, 58.3 us)
Async XLA Ops:
  0.0 38.0 %all-to-all-start = ((bf16[8,32,2048]{2,0,1:T(8,128)(2,1)}), bf16[8,32,2048]{2,0,1:T(8,128)(2,1)S(1)}, u32[]{:S(2)}, u32[]{:S(2)}) async-start(bf16[8,32,2048]{2,0,1:T(8,128)(2,1)} %bitcast.43), calls=%async_computation | async-start | bytes 2097152 | tf_op jit(solution)/shard_map/all_to_all | solution.py:259
  16.1 21.9 %collective-permute-start.5 = (bf16[4,8,256,128]{3,2,1,0:T(8,128)(2,1)}, bf16[4,8,256,128]{3,2,1,0:T(8,128)(2,1)}, u32[]{:S(2)}, u32[]{:S(2)}) collective-permute-start(bf16[4,8,256,128]{3,2,1,0:T(8,128)(2,1)} %get-tuple-element.103), channel_id=1, source_target_pairs={{0,32},{32,0},{64,96},{96,64},{128,160},{160,128},{192,224},{224,1... | collective-permute-start | bytes 6291464 | tf_op jit(solution)/shard_map/ppermute | solution.py:265
  43.8 29.1 %collective-permute-start.16 = (bf16[32,48,128]{2,1,0:T(8,128)(2,1)S(1)}, bf16[32,48,128]{2,1,0:T(8,128)(2,1)S(1)}, u32[]{:S(2)}, u32[]{:S(2)}) collective-permute-start(bf16[32,48,128]{2,1,0:T(8,128)(2,1)S(1)} %get-tuple-element.80), channel_id=1, source_target_pairs={{0,64},{32,96},{64,128},{96,160},{128,192},{160,224},{192,0},{224,... | collective-permute-start | bytes 1179656 | tf_op jit(solution)/shard_map/ppermute | solution.py:178
  45.3 29.3 %collective-permute-start.17 = (bf16[32,48,128]{2,1,0:T(8,128)(2,1)S(1)}, bf16[32,48,128]{2,1,0:T(8,128)(2,1)S(1)}, u32[]{:S(2)}, u32[]{:S(2)}) collective-permute-start(bf16[32,48,128]{2,1,0:T(8,128)(2,1)S(1)} %get-tuple-element.81), channel_id=1, source_target_pairs={{0,128},{32,160},{64,192},{96,224},{128,0},{160,32},{192,64},{224,... | collective-permute-start | bytes 1179656 | tf_op jit(solution)/shard_map/ppermute | solution.py:178
  51.2 19.9 %collective-permute-start.7 = (bf16[32,32,128]{2,1,0:T(8,128)(2,1)S(1)}, bf16[32,32,128]{2,1,0:T(8,128)(2,1)S(1)}, u32[]{:S(2)}, u32[]{:S(2)}) collective-permute-start(bf16[32,32,128]{2,1,0:T(8,128)(2,1)S(1)} %get-tuple-element.65), channel_id=1, source_target_pairs={{0,64},{32,96},{64,128},{96,160},{128,192},{160,224},{192,0},{224,... | collective-permute-start | bytes 786440 | tf_op jit(solution)/shard_map/ppermute | solution.py:178
  51.3 24.9 %collective-permute-start.18 = (bf16[32,48,128]{2,1,0:T(8,128)(2,1)S(1)}, bf16[32,48,128]{2,1,0:T(8,128)(2,1)S(1)}, u32[]{:S(2)}, u32[]{:S(2)}) collective-permute-start(bf16[32,48,128]{2,1,0:T(8,128)(2,1)S(1)} %get-tuple-element.82), channel_id=1, source_target_pairs={{0,192},{32,224},{64,0},{96,32},{128,64},{160,96},{192,128},{224,1... | collective-permute-start | bytes 1179656 | tf_op jit(solution)/shard_map/ppermute | solution.py:178
  54.5 43.1 %collective-permute-start.29 = (bf16[32,48,128]{2,1,0:T(8,128)(2,1)S(1)}, bf16[32,48,128]{2,1,0:T(8,128)(2,1)S(1)}, u32[]{:S(2)}, u32[]{:S(2)}) collective-permute-start(bf16[32,48,128]{2,1,0:T(8,128)(2,1)S(1)} %get-tuple-element.91), channel_id=1, source_target_pairs={{0,64},{32,96},{64,128},{96,160},{128,192},{160,224},{192,0},{224,... | collective-permute-start | bytes 1179656 | tf_op jit(solution)/shard_map/ppermute | solution.py:178
  71.1 29.4 %collective-permute-start.30 = (bf16[32,48,128]{2,1,0:T(8,128)(2,1)S(1)}, bf16[32,48,128]{2,1,0:T(8,128)(2,1)S(1)}, u32[]{:S(2)}, u32[]{:S(2)}) collective-permute-start(bf16[32,48,128]{2,1,0:T(8,128)(2,1)S(1)} %get-tuple-element.92), channel_id=1, source_target_pairs={{0,128},{32,160},{64,192},{96,224},{128,0},{160,32},{192,64},{224,... | collective-permute-start | bytes 1179656 | tf_op jit(solution)/shard_map/ppermute | solution.py:178
  72.9 20.8 %collective-permute-start.8 = (bf16[32,32,128]{2,1,0:T(8,128)(2,1)S(1)}, bf16[32,32,128]{2,1,0:T(8,128)(2,1)S(1)}, u32[]{:S(2)}, u32[]{:S(2)}) collective-permute-start(bf16[32,32,128]{2,1,0:T(8,128)(2,1)S(1)} %get-tuple-element.66), channel_id=1, source_target_pairs={{0,128},{32,160},{64,192},{96,224},{128,0},{160,32},{192,64},{224,... | collective-permute-start | bytes 786440 | tf_op jit(solution)/shard_map/ppermute | solution.py:178
  74.6 20.6 %collective-permute-start.9 = (bf16[32,32,128]{2,1,0:T(8,128)(2,1)S(1)}, bf16[32,32,128]{2,1,0:T(8,128)(2,1)S(1)}, u32[]{:S(2)}, u32[]{:S(2)}) collective-permute-start(bf16[32,32,128]{2,1,0:T(8,128)(2,1)S(1)} %get-tuple-element.67), channel_id=1, source_target_pairs={{0,192},{32,224},{64,0},{96,32},{128,64},{160,96},{192,128},{224,1... | collective-permute-start | bytes 786440 | tf_op jit(solution)/shard_map/ppermute | solution.py:178
  76.2 25.9 %collective-permute-start.31 = (bf16[32,48,128]{2,1,0:T(8,128)(2,1)S(1)}, bf16[32,48,128]{2,1,0:T(8,128)(2,1)S(1)}, u32[]{:S(2)}, u32[]{:S(2)}) collective-permute-start(bf16[32,48,128]{2,1,0:T(8,128)(2,1)S(1)} %get-tuple-element.93), channel_id=1, source_target_pairs={{0,192},{32,224},{64,0},{96,32},{128,64},{160,96},{192,128},{224,1... | collective-permute-start | bytes 1179656 | tf_op jit(solution)/shard_map/ppermute | solution.py:178
  93.8 36.9 %collective-permute-start.19 = (bf16[32,48,128]{2,1,0:T(8,128)(2,1)S(1)}, bf16[32,48,128]{2,1,0:T(8,128)(2,1)S(1)}, u32[]{:S(2)}, u32[]{:S(2)}) collective-permute-start(bf16[32,48,128]{2,1,0:T(8,128)(2,1)S(1)} %get-tuple-element.84), channel_id=1, source_target_pairs={{0,8},{1,9},{2,10},{3,11},{4,12},{5,13},{6,14},{7,15},{8,16},{9,17... | collective-permute-start | bytes 1179656 | tf_op jit(solution)/shard_map/ppermute | solution.py:178
  96.1 16.0 %collective-permute-start.10 = (bf16[32,32,128]{2,1,0:T(8,128)(2,1)S(1)}, bf16[32,32,128]{2,1,0:T(8,128)(2,1)S(1)}, u32[]{:S(2)}, u32[]{:S(2)}) collective-permute-start(bf16[32,32,128]{2,1,0:T(8,128)(2,1)S(1)} %get-tuple-element.69), channel_id=1, source_target_pairs={{0,8},{1,9},{2,10},{3,11},{4,12},{5,13},{6,14},{7,15},{8,16},{9,17... | collective-permute-start | bytes 786440 | tf_op jit(solution)/shard_map/ppermute | solution.py:178
  97.6 30.9 %collective-permute-start.11 = (bf16[32,32,128]{2,1,0:T(8,128)(2,1)S(1)}, bf16[32,32,128]{2,1,0:T(8,128)(2,1)S(1)}, u32[]{:S(2)}, u32[]{:S(2)}) collective-permute-start(bf16[32,32,128]{2,1,0:T(8,128)(2,1)S(1)} %get-tuple-element.70), channel_id=1, source_target_pairs={{0,16},{1,17},{2,18},{3,19},{4,20},{5,21},{6,22},{7,23},{8,24},{9,... | collective-permute-start | bytes 786440 | tf_op jit(solution)/shard_map/ppermute | solution.py:178
  100.5 28.0 %collective-permute-start.12 = (bf16[32,32,128]{2,1,0:T(8,128)(2,1)S(1)}, bf16[32,32,128]{2,1,0:T(8,128)(2,1)S(1)}, u32[]{:S(2)}, u32[]{:S(2)}) collective-permute-start(bf16[32,32,128]{2,1,0:T(8,128)(2,1)S(1)} %get-tuple-element.71), channel_id=1, source_target_pairs={{0,24},{1,25},{2,26},{3,27},{4,28},{5,29},{6,30},{7,31},{8,0},{9,1... | collective-permute-start | bytes 786440 | tf_op jit(solution)/shard_map/ppermute | solution.py:178
  102.1 29.8 %collective-permute-start.20 = (bf16[32,48,128]{2,1,0:T(8,128)(2,1)S(1)}, bf16[32,48,128]{2,1,0:T(8,128)(2,1)S(1)}, u32[]{:S(2)}, u32[]{:S(2)}) collective-permute-start(bf16[32,48,128]{2,1,0:T(8,128)(2,1)S(1)} %get-tuple-element.85), channel_id=1, source_target_pairs={{0,16},{1,17},{2,18},{3,19},{4,20},{5,21},{6,22},{7,23},{8,24},{9,... | collective-permute-start | bytes 1179656 | tf_op jit(solution)/shard_map/ppermute | solution.py:178
  112.1 23.2 %collective-permute-start.21 = (bf16[32,48,128]{2,1,0:T(8,128)(2,1)S(1)}, bf16[32,48,128]{2,1,0:T(8,128)(2,1)S(1)}, u32[]{:S(2)}, u32[]{:S(2)}) collective-permute-start(bf16[32,48,128]{2,1,0:T(8,128)(2,1)S(1)} %get-tuple-element.86), channel_id=1, source_target_pairs={{0,24},{1,25},{2,26},{3,27},{4,28},{5,29},{6,30},{7,31},{8,0},{9,1... | collective-permute-start | bytes 1179656 | tf_op jit(solution)/shard_map/ppermute | solution.py:178
  132.0 30.1 %collective-permute-start.13 = (bf16[64,32,128]{2,1,0:T(8,128)(2,1)S(1)}, bf16[64,32,128]{2,1,0:T(8,128)(2,1)S(1)}, u32[]{:S(2)}, u32[]{:S(2)}) collective-permute-start(bf16[64,32,128]{2,1,0:T(8,128)(2,1)S(1)} %get-tuple-element.73), channel_id=1, source_target_pairs={{0,1},{1,0},{2,3},{3,2},{4,5},{5,4},{6,7},{7,6},{8,9},{9,8},{10,11... | collective-permute-start | bytes 1572872 | tf_op jit(solution)/shard_map/ppermute | solution.py:307
  162.2 21.3 %collective-permute-start.14 = (bf16[32,32,128]{2,1,0:T(8,128)(2,1)S(1)}, bf16[32,32,128]{2,1,0:T(8,128)(2,1)S(1)}, u32[]{:S(2)}, u32[]{:S(2)}) collective-permute-start(bf16[32,32,128]{2,1,0:T(8,128)(2,1)S(1)} %get-tuple-element.75), channel_id=1, source_target_pairs={{0,2},{1,3},{2,0},{3,1},{4,6},{5,7},{6,4},{7,5},{8,10},{9,11},{10,... | collective-permute-start | bytes 786440 | tf_op jit(solution)/shard_map/ppermute | solution.py:307
  163.9 16.1 %collective-permute-start.24 = (bf16[16,48,128]{2,1,0:T(8,128)(2,1)S(1)}, bf16[16,48,128]{2,1,0:T(8,128)(2,1)S(1)}, u32[]{:S(2)}, u32[]{:S(2)}) collective-permute-start(bf16[16,48,128]{2,1,0:T(8,128)(2,1)S(1)} %shard_map.74), channel_id=1, source_target_pairs={{0,1},{1,2},{2,3},{3,4},{4,5},{5,6},{6,7},{7,0},{8,9},{9,10},{10,1... | collective-permute-start | bytes 589832 | tf_op jit(solution)/shard_map/ppermute | solution.py:244
  167.2 15.4 %collective-permute-start.40 = (bf16[16,48,128]{2,1,0:T(8,128)(2,1)S(1)}, bf16[16,48,128]{2,1,0:T(8,128)(2,1)S(1)}, u32[]{:S(2)}, u32[]{:S(2)}) collective-permute-start(bf16[16,48,128]{2,1,0:T(8,128)(2,1)S(1)} %shard_map.83), channel_id=1, source_target_pairs={{0,7},{1,0},{2,1},{3,2},{4,3},{5,4},{6,5},{7,6},{8,15},{9,8},{10,9... | collective-permute-start | bytes 589832 | tf_op jit(solution)/shard_map/ppermute | solution.py:244
  167.9 19.4 %collective-permute-start.28 = (bf16[16,48,128]{2,1,0:T(8,128)(2,1)S(1)}, bf16[16,48,128]{2,1,0:T(8,128)(2,1)S(1)}, u32[]{:S(2)}, u32[]{:S(2)}) collective-permute-start(bf16[16,48,128]{2,1,0:T(8,128)(2,1)S(1)} %shard_map.77), channel_id=1, source_target_pairs={{0,7},{1,0},{2,1},{3,2},{4,3},{5,4},{6,5},{7,6},{8,15},{9,8},{10,9... | collective-permute-start | bytes 589832 | tf_op jit(solution)/shard_map/ppermute | solution.py:244
  171.1 16.2 %collective-permute-start.37 = (bf16[16,48,128]{2,1,0:T(8,128)(2,1)S(1)}, bf16[16,48,128]{2,1,0:T(8,128)(2,1)S(1)}, u32[]{:S(2)}, u32[]{:S(2)}) collective-permute-start(bf16[16,48,128]{2,1,0:T(8,128)(2,1)S(1)} %shard_map.81), channel_id=1, source_target_pairs={{0,1},{1,2},{2,3},{3,4},{4,5},{5,6},{6,7},{7,0},{8,9},{9,10},{10,1... | collective-permute-start | bytes 589832 | tf_op jit(solution)/shard_map/ppermute | solution.py:244
  180.0 14.8 %collective-permute-start.25 = (bf16[16,48,128]{2,1,0:T(8,128)(2,1)S(1)}, bf16[16,48,128]{2,1,0:T(8,128)(2,1)S(1)}, u32[]{:S(2)}, u32[]{:S(2)}) collective-permute-start(bf16[16,48,128]{2,1,0:T(8,128)(2,1)S(1)} %shard_map.75), channel_id=1, source_target_pairs={{0,1},{1,2},{2,3},{3,4},{4,5},{5,6},{6,7},{7,0},{8,9},{9,10},{10,1... | collective-permute-start | bytes 589832 | tf_op jit(solution)/shard_map/ppermute | solution.py:244
  (23 other events, 247.2 us)
